TPU v7x, 32 devices: a whole 2x2x4 slice. The times are simulated.
32 devices in a mesh: seq: 8 (over z, core), fsdp: 4 (over y, x).
Axes of the slice: x: 2, y: 2, z: 4, core: 2. Of those that a mesh axis runs over, the one named last changes fastest.
Arguments:
- signal: bfloat16 [4, 8192, 1024], P('fsdp', 'seq'), may hold values from -6 to 6
- cotangent: bfloat16 [4, 8192, 1024], P('fsdp', 'seq'), may hold values from -6 to 6
- w_in: bfloat16 [1024, 1024], P('fsdp'), may hold values from -0.1875 to 0.1875
- w_conv: bfloat16 [2, 1024, 128], P(None, 'seq'), may hold values from -0.5 to 0.5
- w_out: bfloat16 [1024, 1024], P('fsdp'), may hold values from -0.1875 to 0.1875
- dilation: int32 [16], P('seq'), may hold values from 512 to 4095
- lengths: int32 [4], P('fsdp'), may hold values from 2048 to 8192, as said below
Outputs:
- grad_signal: bfloat16 [4, 8192, 1024], P('fsdp', 'seq')
- grad_in: float32 [1024, 1024], P('fsdp')
- grad_out: float32 [1024, 1024], P('fsdp')
- grad_conv: float32 [2, 1024, 128], P(None, 'seq')
Inputs may be any that keep to these rules, and one draw needn't show every extreme that they name: `lengths`: some record in every draw holds all 8192 samples.
All inputs are finite; a program needn't handle non-finite values.
Results may differ from a plain program's by a relative error of at most 0.0068.
Values may be sent and summed in bfloat16 or wider, within the bound.
No kernel may reach another device: no remote copies, remote signals or barrier semaphores. Data moves between devices by JAX's collectives and lax.ppermute only.
A program may use at most 128 MiB of HBM per device.

v0:
```python
import math
import jax
import jax.numpy as jnp
from jax import lax
from jax.sharding import PartitionSpec as P


def delayed(series, amount):
    padded = jnp.concatenate([jnp.zeros_like(series), series], axis=0)
    return lax.dynamic_slice_in_dim(padded, series.shape[0] - amount, series.shape[0], 0)


def advanced(series, amount):
    padded = jnp.concatenate([series, jnp.zeros_like(series)], axis=0)
    return lax.dynamic_slice_in_dim(padded, amount, series.shape[0], 0)


def group_pass(projected, grad_gated, kernel, amount, live_mask):
    group_width = kernel.shape[0] // 2
    stacked = jnp.concatenate([projected, delayed(projected, amount)], axis=1)
    pre_acts = jnp.dot(stacked, kernel, preferred_element_type=jnp.float32)
    tanh_act = jnp.tanh(pre_acts[:, :group_width])
    sig_act = jax.nn.sigmoid(pre_acts[:, group_width:])
    masked = live_mask[:, None]
    gated_out = (tanh_act * sig_act * masked).astype(jnp.bfloat16)
    grad_masked = grad_gated.astype(jnp.float32) * masked
    grad_filter = grad_masked * sig_act * (1.0 - tanh_act * tanh_act)
    grad_gate = grad_masked * tanh_act * sig_act * (1.0 - sig_act)
    grad_acts = jnp.concatenate([grad_filter, grad_gate], axis=1).astype(jnp.bfloat16)
    grad_kernel = jnp.dot(stacked.T, grad_acts, preferred_element_type=jnp.float32)
    paired = jnp.concatenate([grad_acts, advanced(grad_acts, amount)], axis=1)
    back_kernel = jnp.concatenate([kernel[:group_width].T, kernel[group_width:].T], axis=0)
    grad_mixed = jnp.dot(paired, back_kernel, preferred_element_type=jnp.float32).astype(
        jnp.bfloat16
    )
    return (gated_out, grad_mixed, grad_kernel)


def column_order(series, fsdp_size, seq_size):
    samples, channels = series.shape
    quarter = channels // (fsdp_size * seq_size)
    return (
        series.reshape(samples, fsdp_size, seq_size, quarter)
        .transpose(0, 2, 1, 3)
        .reshape(samples, channels)
    )


def outer_terms(left_side, right_side):
    return lax.dot_general(
        left_side, right_side, (((0,), (0,)), ((), ())), preferred_element_type=jnp.float32
    )


def local(signal, cotangent, w_in, w_conv, w_out, dilation, lengths):
    record = signal[0]
    upstream = cotangent[0]
    samples, channels = record.shape
    seq_size = lax.axis_size("seq")
    fsdp_size = lax.axis_size("fsdp")
    full_len = samples * seq_size
    local_groups = dilation.shape[0]
    local_chans = w_conv.shape[1]
    group_width = local_chans // local_groups
    factor = 1.0 / math.sqrt(full_len * fsdp_size)
    projected = jnp.dot(
        record, lax.all_gather(w_in, "fsdp", axis=0, tiled=True), preferred_element_type=jnp.float32
    ).astype(jnp.bfloat16)
    grad_gated = lax.dot_general(
        upstream,
        lax.all_gather(w_out, "fsdp", axis=0, tiled=True),
        (((1,), (1,)), ((), ())),
        preferred_element_type=jnp.float32,
    ).astype(jnp.bfloat16)
    proj_groups, grad_groups = (
        lax.all_to_all(projected, "seq", split_axis=1, concat_axis=0, tiled=True),
        lax.all_to_all(grad_gated, "seq", split_axis=1, concat_axis=0, tiled=True),
    )
    live_mask = (jnp.arange(full_len, dtype=jnp.int32) < lengths[0]).astype(jnp.float32)
    gated_parts = []
    mixed_parts = []
    tap_zero = []
    tap_one = []
    for group_index in range(local_groups):
        low_chan = group_index * group_width
        kernel = jnp.concatenate(
            [
                w_conv[0, low_chan : low_chan + group_width],
                w_conv[1, low_chan : low_chan + group_width],
            ],
            axis=0,
        )
        gated_out, grad_mixed, grad_kernel = group_pass(
            proj_groups[:, low_chan : low_chan + group_width],
            grad_groups[:, low_chan : low_chan + group_width],
            kernel,
            dilation[group_index],
            live_mask,
        )
        gated_parts.append(gated_out)
        mixed_parts.append(grad_mixed)
        tap_zero.append(grad_kernel[:group_width])
        tap_one.append(grad_kernel[group_width:])
    gated_groups = jnp.concatenate(gated_parts, axis=1)
    mixed_groups = jnp.concatenate(mixed_parts, axis=1)
    conv_local = jnp.stack(
        [jnp.concatenate(tap_zero, axis=0), jnp.concatenate(tap_one, axis=0)], axis=0
    )
    conv_total = lax.psum(conv_local, "fsdp")
    gated_time, mixed_time = (
        lax.all_to_all(gated_groups, "seq", split_axis=0, concat_axis=1, tiled=True),
        lax.all_to_all(mixed_groups, "seq", split_axis=0, concat_axis=1, tiled=True),
    )
    mixed_back = lax.dot_general(
        mixed_time,
        lax.all_gather(w_in, "fsdp", axis=0, tiled=True),
        (((1,), (1,)), ((), ())),
        preferred_element_type=jnp.float32,
    )
    grad_signal = (upstream.astype(jnp.float32) + mixed_back).astype(jnp.bfloat16)[None]
    gated_order = column_order(gated_time, fsdp_size, seq_size)
    record_order = column_order(record, fsdp_size, seq_size)
    part_out = lax.psum_scatter(
        outer_terms(gated_order, upstream), ("seq", "fsdp"), scatter_dimension=0, tiled=True
    )
    part_in = lax.psum_scatter(
        outer_terms(record_order, mixed_time), ("seq", "fsdp"), scatter_dimension=0, tiled=True
    )
    grad_in, grad_out = (
        lax.all_gather(part_in, "seq", axis=0, tiled=True),
        lax.all_gather(part_out, "seq", axis=0, tiled=True),
    )
    return (grad_signal, grad_in * factor, grad_out * factor, conv_total * factor)


def solution(mesh):
    placed = (
        P("fsdp", "seq", None),
        P("fsdp", "seq", None),
        P("fsdp", None),
        P(None, "seq", None),
        P("fsdp", None),
        P("seq"),
        P("fsdp"),
    )
    return jax.shard_map(
        local,
        mesh=mesh,
        in_specs=placed,
        out_specs=(P("fsdp", "seq", None), P("fsdp", None), P("fsdp", None), P(None, "seq", None)),
        check_vma=False,
    )
```

profile of v0, /device:TPU:0, one launch (start us, length us, event | category | flops | bytes accessed | tf_op | source)
XLA Modules:
  0.0 627.7 jit_solution(6793822717476289242)
XLA Ops:
  8.6 39.1 %all-gather.7.cloned.1.call-done = bf16[1024,1024]{1,0:T(8,128)(2,1)} async-done(((bf16[256,1024]{1,0:T(8,128)(2,1)}), bf16[1024,1024]{1,0:T(8,128)(2,1)}) %all-gather.7.cloned.1.call-update) | async-done | bytes 2097168 | tf_op jit(solution)/shard_map/all_gather | solution.py:67
  47.8 4.6 fusion.26
  52.4 2.4 copy.26
  54.7 4.6 all-to-all-start.1
  59.3 25.5 %all-gather.5.cloned.1.call-done = bf16[1024,1024]{1,0:T(8,128)(2,1)} async-done(((bf16[256,1024]{1,0:T(8,128)(2,1)}), bf16[1024,1024]{1,0:T(8,128)(2,1)}) %all-gather.5.cloned.1.call-update) | async-done | bytes 2097168 | tf_op jit(solution)/shard_map/all_gather | solution.py:71
  84.8 6.0 fusion.23
  90.8 17.6 %all-to-all-done.1 = bf16[1024,8,128]{2,0,1:T(8,128)(2,1)S(1)} async-done(((bf16[1024,8,128]{2,0,1:T(8,128)(2,1)}), bf16[1024,8,128]{2,0,1:T(8,128)(2,1)S(1)}, u32[]{:S(2)}, u32[]{:S(2)}) %all-to-all-start.1) | async-done | bytes 2097184 | tf_op jit(solution)/shard_map/all_to_all | solution.py:76
  108.4 4.7 all-to-all-start
  116.7 2.7 fusion.52
  119.4 42.5 %all-to-all-done = bf16[1024,8,128]{0,2,1:T(8,128)(2,1)} async-done(((bf16[1024,8,128]{0,2,1:T(8,128)(2,1)}), bf16[1024,8,128]{0,2,1:T(8,128)(2,1)}, u32[]{:S(2)}, u32[]{:S(2)}) %all-to-all-start) | async-done | bytes 2097184 | tf_op jit(solution)/shard_map/all_to_all | solution.py:77
  164.8 8.6 %pad_dynamic-slice_fusion.1 = (bf16[8192,64]{1,0:T(8,128)(2,1)S(1)}, bf16[8192,64]{1,0:T(8,128)(2,1)S(1)}) fusion(s32[]{:T(128)S(6)} %select_n.14, bf16[8192,64]{1,0:T(8,128)(2,1)S(1)} %copy-done, s32[]{:T(128)S(6)} %select_n.12, bf16[8192,64]{1,0:T(8,128)(2,1)S(1)} %copy-done.1), kind=kLoop, calls=%fused_computation.14 | loop fusion | bytes 4194312 | tf_op jit(solution)/shard_map/dynamic_slice | solution.py:10
  176.9 3.7 multiply_convert_fusion.3
  182.3 4.3 all-to-all-start.3
  190.3 3.1 pad_maximum_fusion.1
  193.4 42.3 %all-to-all-done.3 = bf16[8,1024,128]{1,2,0:T(8,128)(2,1)} async-done(((bf16[8,1024,128]{1,2,0:T(8,128)(2,1)}), bf16[8,1024,128]{1,2,0:T(8,128)(2,1)}, u32[]{:S(2)}, u32[]{:S(2)}) %all-to-all-start.3) | async-done | bytes 2097184 | tf_op jit(solution)/shard_map/all_to_all | solution.py:111
  237.9 4.3 fusion.19
  242.3 2.4 pad_dynamic-slice_fusion.2
  249.8 4.4 all-to-all-start.2
  254.2 4.0 copy.28
  258.2 3.3 copy.29
  261.4 49.1 %all-to-all-done.2 = bf16[8,1024,128]{1,2,0:T(8,128)(2,1)} async-done(((bf16[8,1024,128]{1,2,0:T(8,128)(2,1)}), bf16[8,1024,128]{1,2,0:T(8,128)(2,1)}, u32[]{:S(2)}, u32[]{:S(2)}) %all-to-all-start.2) | async-done | bytes 2097184 | tf_op jit(solution)/shard_map/all_to_all | solution.py:112
  310.5 6.6 %convolution_bitcast_fusion = f32[1024,1024]{0,1:T(8,128)} fusion(bf16[1024,1024]{0,1:T(8,128)(2,1)} %bitcast.20, bf16[1024,1024]{0,1:T(8,128)(2,1)} %bitcast.91), kind=kOutput, calls=%fused_computation.17 | convolution fusion | flops 2147483648 | bytes 8388608 | tf_op jit(solution)/shard_map/dot_general | solution.py:50
  317.1 5.5 copy.36
  323.0 4.5 fusion.31
  329.9 56.5 %reduce-scatter.9.cloned.1.call-done = f32[32,1024]{1,0:T(8,128)} async-done(((f32[1024,1024]{1,0:T(8,128)}), f32[32,1024]{1,0:T(8,128)}) %reduce-scatter.9.cloned.1.call-update) | async-done | bytes 131088 | tf_op jit(solution)/shard_map/reduce_scatter | solution.py:123
  386.5 142.3 %reduce-scatter.7.cloned.1.call-done = f32[32,1024]{1,0:T(8,128)} async-done(((f32[1024,1024]{1,0:T(8,128)}), f32[32,1024]{1,0:T(8,128)}) %reduce-scatter.7.cloned.1.call-update) | async-done | bytes 131088 | tf_op jit(solution)/shard_map/reduce_scatter | solution.py:126
  528.8 42.5 %all-reduce.6.cloned.1.call-done = f32[2,128,128]{2,1,0:T(8,128)} async-done(((f32[2,128,128]{2,1,0:T(8,128)}), f32[2,128,128]{2,1,0:T(8,128)}) %all-reduce.6.cloned.1.call-update) | async-done | bytes 131088 | tf_op jit(solution)/shard_map/psum | solution.py:109
  572.9 6.6 %fusion.10 = bf16[1,1024,1024]{2,1,0:T(8,128)(2,1)} fusion(bf16[1,1024,1024]{2,1,0:T(8,128)(2,1)} %param.8, bf16[1024,1024]{0,1:T(8,128)(2,1)} %bitcast.20, bf16[1024,1024]{1,0:T(8,128)(2,1)} %all-gather.7.cloned.1.call-done), kind=kOutput, calls=%fused_computation.18 | convolution fusion | flops 2150629376 | bytes 8388608 | tf_op jit(solution)/shard_map/dot_general | solution.py:114
  579.5 15.6 %all-gather.11.cloned.1.call-done = f32[256,1024]{1,0:T(8,128)} async-done(((f32[32,1024]{1,0:T(8,128)}), f32[256,1024]{1,0:T(8,128)}) %all-gather.11.cloned.1.call-update) | async-done | bytes 1048592 | tf_op jit(solution)/shard_map/all_gather | solution.py:131
  595.1 2.3 broadcast_multiply_fusion
  597.4 21.1 %all-gather.9.cloned.1.call-done = f32[256,1024]{1,0:T(8,128)} async-done(((f32[32,1024]{1,0:T(8,128)}), f32[256,1024]{1,0:T(8,128)}) %all-gather.9.cloned.1.call-update) | async-done | bytes 1048592 | tf_op jit(solution)/shard_map/all_gather | solution.py:130
  618.5 2.3 broadcast_multiply_fusion.1
  (60 shorter events, 21.7 us)
Async XLA Ops:
  7.2 40.6 %all-gather.7.cloned.1.call-start = ((), (), s32[]{:S(2)}) async-start(), calls=%async_computation.7 | async-start | bytes 2621440 | tf_op jit(solution)/shard_map/all_gather | solution.py:67
  7.9 76.9 %all-gather.5.cloned.1.call-start = ((), (), s32[]{:S(2)}) async-start(), calls=%async_computation.6 | async-start | bytes 2621440 | tf_op jit(solution)/shard_map/all_gather | solution.py:71
  54.7 53.6 %all-to-all-start.1 = ((bf16[1024,8,128]{2,0,1:T(8,128)(2,1)}), bf16[1024,8,128]{2,0,1:T(8,128)(2,1)S(1)}, u32[]{:S(2)}, u32[]{:S(2)}) async-start(bf16[1024,8,128]{2,0,1:T(8,128)(2,1)} %copy.26), calls=%async_computation.1 | async-start | bytes 4194304 | tf_op jit(solution)/shard_map/all_to_all | solution.py:76
  108.4 4.7 copy-start.10
  108.4 8.3 %copy-start.9 = (bf16[2,128,128]{2,1,0:T(8,128)(2,1)S(1)}, bf16[2,128,128]{2,1,0:T(8,128)(2,1)}, u32[]{:S(2)}) copy-start(bf16[2,128,128]{2,1,0:T(8,128)(2,1)} %param.10) | copy-start | bytes 196612
  108.4 53.5 %all-to-all-start = ((bf16[1024,8,128]{0,2,1:T(8,128)(2,1)}), bf16[1024,8,128]{0,2,1:T(8,128)(2,1)}, u32[]{:S(2)}, u32[]{:S(2)}) async-start(bf16[1024,8,128]{0,2,1:T(8,128)(2,1)} %bitcast.90), calls=%async_computation | async-start | bytes 4194304 | tf_op jit(solution)/shard_map/all_to_all | solution.py:77
  161.9 2.2 copy-start
  161.9 2.9 copy-start.1
  173.4 1.4 copy-start.4
  173.4 2.0 copy-start.2
  182.3 53.4 %all-to-all-start.3 = ((bf16[8,1024,128]{1,2,0:T(8,128)(2,1)}), bf16[8,1024,128]{1,2,0:T(8,128)(2,1)}, u32[]{:S(2)}, u32[]{:S(2)}) async-start(bf16[8,1024,128]{1,2,0:T(8,128)(2,1)} %bitcast.84), calls=%async_computation.3 | async-start | bytes 4194304 | tf_op jit(solution)/shard_map/all_to_all | solution.py:111
  186.7 199.8 %reduce-scatter.9.cloned.1.call-start = ((), (), s32[]{:S(2)}) async-start(), calls=%async_computation.12 | async-start | bytes 4325376 | tf_op jit(solution)/shard_map/reduce_scatter | solution.py:123
  235.7 2.2 copy-start.11
  242.3 2.5 copy-start.7
  242.3 2.5 copy-start.8
  244.7 1.2 copy-start.5
  249.8 60.8 %all-to-all-start.2 = ((bf16[8,1024,128]{1,2,0:T(8,128)(2,1)}), bf16[8,1024,128]{1,2,0:T(8,128)(2,1)}, u32[]{:S(2)}, u32[]{:S(2)}) async-start(bf16[8,1024,128]{1,2,0:T(8,128)(2,1)} %bitcast.85), calls=%async_computation.2 | async-start | bytes 4194304 | tf_op jit(solution)/shard_map/all_to_all | solution.py:112
  254.1 274.7 %reduce-scatter.7.cloned.1.call-start = ((), (), s32[]{:S(2)}) async-start(), calls=%async_computation.11 | async-start | bytes 4325376 | tf_op jit(solution)/shard_map/reduce_scatter | solution.py:126
  322.7 248.7 %all-reduce.6.cloned.1.call-start = ((), (), s32[]{:S(2)}) async-start(), calls=%async_computation.10 | async-start | bytes 262144 | tf_op jit(solution)/shard_map/psum | solution.py:109
  323.0 4.5 copy-start.3
  323.0 4.5 copy-start.6
  329.9 265.2 %all-gather.11.cloned.1.call-start = ((), (), s32[]{:S(2)}) async-start(), calls=%async_computation.9 | async-start | bytes 1179648 | tf_op jit(solution)/shard_map/all_gather | solution.py:131
  386.5 232.0 %all-gather.9.cloned.1.call-start = ((), (), s32[]{:S(2)}) async-start(), calls=%async_computation.8 | async-start | bytes 1179648 | tf_op jit(solution)/shard_map/all_gather | solution.py:130
Sparse Core Ops, SparseCore 0:
  9.8 37.8 all-gather.6
  49.6 35.1 all-gather.4
  242.4 144.0 reduce-scatter.8
  388.6 140.1 reduce-scatter.6
  532.1 39.1 all-reduce.5
  572.8 22.2 all-gather.10
  596.7 21.8 all-gather.8
where the time goes:
time: 629 us; the launch traced here: 628 us
  waiting for transfers between devices  496 us (79%)
  local copies, waits for them, and re-layouts  39.4 us (6%)
  matrix products  38.9 us (6%)
  between operations  21 us (3%)
  starting transfers between devices  18.5 us (3%)
  other arithmetic  14.3 us (2%)
    reduce_scatter x1, waiting for transfers between devices, local(): lax.psum_scatter(outer_terms(record_order, mixed_time), ('seq', 'fsdp'),...  142 us
    reduce_scatter x1, waiting for transfers between devices, local(): lax.psum_scatter(outer_terms(gated_order, upstream), ('seq', 'fsdp'), sca...  56.5 us
    all_to_all x1, waiting for transfers between devices, local(): lax.all_to_all(mixed_groups, 'seq', split_axis=0, concat_axis=1, tiled=True)  49.1 us
    psum x1, waiting for transfers between devices, local(): conv_total = lax.psum(conv_local, 'fsdp')  42.5 us
    all_to_all x1, waiting for transfers between devices, local(): lax.all_to_all(grad_gated, 'seq', split_axis=1, concat_axis=0, tiled=True)  42.5 us
    all_to_all x1, waiting for transfers between devices, local(): lax.all_to_all(gated_groups, 'seq', split_axis=0, concat_axis=1, tiled=True)  42.3 us
    all_gather x1, waiting for transfers between devices, local(): lax.all_gather(w_in, 'fsdp', axis=0, tiled=True)  39.1 us
    all_gather x1, waiting for transfers between devices, local(): lax.all_gather(w_out, 'fsdp', axis=0, tiled=True)  25.5 us
  transfers between devices with their start and end apart: 11, of which 11 were waited for; matrix products, arithmetic and copies ran while one was open for 10% of the time, Pallas kernels for 0%

commit v1 on v0

--- a/solution.py
+++ b/solution.py
@@ -106,7 +106,7 @@
     conv_local = jnp.stack(
         [jnp.concatenate(tap_zero, axis=0), jnp.concatenate(tap_one, axis=0)], axis=0
     )
-    conv_total = lax.psum(conv_local, "fsdp")
+    conv_total = jnp.sum(lax.all_gather(conv_local, "fsdp"), axis=0)
     gated_time, mixed_time = (
         lax.all_to_all(gated_groups, "seq", split_axis=0, concat_axis=1, tiled=True),
         lax.all_to_all(mixed_groups, "seq", split_axis=0, concat_axis=1, tiled=True),

time: 629 us -> 582 us (0.925)
  waiting for transfers between devices: 496 us -> 441 us
  blocking collectives: 0 us -> 8.53 us
    psum x1 -> x0, waiting for transfers between devices: 42.5 us -> none  [local(): conv_total = lax.psum(conv_local, 'fsdp')]
    all_gather x1, waiting for transfers between devices: 15.6 us -> 4.05 us  [local(): lax.all_gather(part_out, 'seq', axis=0, tiled=True)]
    all_gather x0 -> x1, blocking collectives: none -> 8.53 us  [local(): conv_total = jnp.sum(lax.all_gather(conv_local, 'fsdp'), axis=0)]
    reduce_scatter x1, waiting for transfers between devices: 56.5 us -> 63.7 us  [local(): lax.psum_scatter(outer_terms(gated_order, upstream), ('seq', 'fsdp'), sca...]
    reduce_scatter x1, waiting for transfers between devices: 142 us -> 136 us  [local(): lax.psum_scatter(outer_terms(record_order, mixed_time), ('seq', 'fsdp'),...]
  transfers between devices with their start and end apart: 11 -> 10, of which waited for: 11 -> 10; matrix products, arithmetic and copies ran while one was open for 10% -> 11% of each run, Pallas kernels for 0% -> 0%
where the time goes in v1:
time: 582 us; the launch traced here: 581 us
  waiting for transfers between devices  441 us (76%)
  local copies, waits for them, and re-layouts  39.5 us (7%)
  matrix products  38.9 us (7%)
  between operations  21.7 us (4%)
  starting transfers between devices  18.5 us (3%)
  other arithmetic  12.8 us (2%)
  blocking collectives  8.53 us (1%)
    reduce_scatter x1, waiting for transfers between devices, local(): lax.psum_scatter(outer_terms(record_order, mixed_time), ('seq', 'fsdp'),...  136 us
    reduce_scatter x1, waiting for transfers between devices, local(): lax.psum_scatter(outer_terms(gated_order, upstream), ('seq', 'fsdp'), sca...  63.7 us
    all_to_all x1, waiting for transfers between devices, local(): lax.all_to_all(mixed_groups, 'seq', split_axis=0, concat_axis=1, tiled=True)  49.1 us
    all_to_all x1, waiting for transfers between devices, local(): lax.all_to_all(grad_gated, 'seq', split_axis=1, concat_axis=0, tiled=True)  42.1 us
    all_to_all x1, waiting for transfers between devices, local(): lax.all_to_all(gated_groups, 'seq', split_axis=0, concat_axis=1, tiled=True)  41.9 us
    all_gather x1, waiting for transfers between devices, local(): lax.all_gather(w_in, 'fsdp', axis=0, tiled=True)  39.1 us
    all_gather x1, waiting for transfers between devices, local(): lax.all_gather(w_out, 'fsdp', axis=0, tiled=True)  25.5 us
    all_gather x1, waiting for transfers between devices, local(): lax.all_gather(part_in, 'seq', axis=0, tiled=True)  21 us
  transfers between devices with their start and end apart: 10, of which 10 were waited for; matrix products, arithmetic and copies ran while one was open for 11% of the time, Pallas kernels for 0%

profile of v1, /device:TPU:0, one launch (start us, length us, event | category | flops | bytes accessed | tf_op | source)
XLA Modules:
  0.0 581.2 jit_solution(7598705660194259229)
XLA Ops:
  8.6 39.1 %all-gather.8.cloned.1.call-done = bf16[1024,1024]{1,0:T(8,128)(2,1)} async-done(((bf16[256,1024]{1,0:T(8,128)(2,1)}), bf16[1024,1024]{1,0:T(8,128)(2,1)}) %all-gather.8.cloned.1.call-update) | async-done | bytes 2097168 | tf_op jit(solution)/shard_map/all_gather | solution.py:67
  47.8 4.6 fusion.26
  52.4 2.4 copy.26
  54.7 4.6 all-to-all-start.1
  59.3 25.5 %all-gather.6.cloned.1.call-done = bf16[1024,1024]{1,0:T(8,128)(2,1)} async-done(((bf16[256,1024]{1,0:T(8,128)(2,1)}), bf16[1024,1024]{1,0:T(8,128)(2,1)}) %all-gather.6.cloned.1.call-update) | async-done | bytes 2097168 | tf_op jit(solution)/shard_map/all_gather | solution.py:71
  84.8 5.9 %fusion.23 = bf16[1024,1024]{0,1:T(8,128)(2,1)} fusion(bf16[1024,1024]{1,0:T(8,128)(2,1)} %all-gather.6.cloned.1.call-done, bf16[1,1024,1024]{2,1,0:T(8,128)(2,1)} %param.8), kind=kOutput, calls=%fused_computation.51 | convolution fusion | flops 2148532224 | bytes 6291456 | tf_op jit(solution)/shard_map/dot_general | solution.py:69
  90.7 17.6 %all-to-all-done.1 = bf16[1024,8,128]{2,0,1:T(8,128)(2,1)S(1)} async-done(((bf16[1024,8,128]{2,0,1:T(8,128)(2,1)}), bf16[1024,8,128]{2,0,1:T(8,128)(2,1)S(1)}, u32[]{:S(2)}, u32[]{:S(2)}) %all-to-all-start.1) | async-done | bytes 2097184 | tf_op jit(solution)/shard_map/all_to_all | solution.py:76
  108.4 4.7 all-to-all-start
  117.1 2.7 fusion.52
  119.8 42.1 %all-to-all-done = bf16[1024,8,128]{0,2,1:T(8,128)(2,1)} async-done(((bf16[1024,8,128]{0,2,1:T(8,128)(2,1)}), bf16[1024,8,128]{0,2,1:T(8,128)(2,1)}, u32[]{:S(2)}, u32[]{:S(2)}) %all-to-all-start) | async-done | bytes 2097184 | tf_op jit(solution)/shard_map/all_to_all | solution.py:77
  164.8 8.6 %pad_dynamic-slice_fusion.1 = (bf16[8192,64]{1,0:T(8,128)(2,1)S(1)}, bf16[8192,64]{1,0:T(8,128)(2,1)S(1)}) fusion(s32[]{:T(128)S(6)} %select_n.14, bf16[8192,64]{1,0:T(8,128)(2,1)S(1)} %copy-done, s32[]{:T(128)S(6)} %select_n.12, bf16[8192,64]{1,0:T(8,128)(2,1)S(1)} %copy-done.1), kind=kLoop, calls=%fused_computation.14 | loop fusion | bytes 4194312 | tf_op jit(solution)/shard_map/dynamic_slice | solution.py:10
  176.9 3.7 multiply_convert_fusion.3
  182.3 4.3 all-to-all-start.3
  190.7 3.1 pad_maximum_fusion.1
  193.8 41.9 %all-to-all-done.3 = bf16[8,1024,128]{1,2,0:T(8,128)(2,1)} async-done(((bf16[8,1024,128]{1,2,0:T(8,128)(2,1)}), bf16[8,1024,128]{1,2,0:T(8,128)(2,1)}, u32[]{:S(2)}, u32[]{:S(2)}) %all-to-all-start.3) | async-done | bytes 2097184 | tf_op jit(solution)/shard_map/all_to_all | solution.py:111
  237.9 4.3 fusion.19
  242.3 2.4 pad_dynamic-slice_fusion.2
  249.7 4.4 all-to-all-start.2
  254.1 4.0 copy.28
  258.1 3.3 copy.29
  261.4 49.1 %all-to-all-done.2 = bf16[8,1024,128]{1,2,0:T(8,128)(2,1)} async-done(((bf16[8,1024,128]{1,2,0:T(8,128)(2,1)}), bf16[8,1024,128]{1,2,0:T(8,128)(2,1)}, u32[]{:S(2)}, u32[]{:S(2)}) %all-to-all-start.2) | async-done | bytes 2097184 | tf_op jit(solution)/shard_map/all_to_all | solution.py:112
  310.5 6.6 %convolution_bitcast_fusion = f32[1024,1024]{0,1:T(8,128)} fusion(bf16[1024,1024]{0,1:T(8,128)(2,1)} %bitcast.20, bf16[1024,1024]{0,1:T(8,128)(2,1)} %bitcast.93), kind=kOutput, calls=%fused_computation.17 | convolution fusion | flops 2147483648 | bytes 8388608 | tf_op jit(solution)/shard_map/dot_general | solution.py:50
  317.1 5.5 copy.36
  322.7 63.7 %reduce-scatter.9.cloned.1.call-done = f32[32,1024]{1,0:T(8,128)} async-done(((f32[1024,1024]{1,0:T(8,128)}), f32[32,1024]{1,0:T(8,128)}) %reduce-scatter.9.cloned.1.call-update) | async-done | bytes 131088 | tf_op jit(solution)/shard_map/reduce_scatter | solution.py:123
  386.8 4.5 fusion.31
  392.9 135.8 %reduce-scatter.7.cloned.1.call-done = f32[32,1024]{1,0:T(8,128)} async-done(((f32[1024,1024]{1,0:T(8,128)}), f32[32,1024]{1,0:T(8,128)}) %reduce-scatter.7.cloned.1.call-update) | async-done | bytes 131088 | tf_op jit(solution)/shard_map/reduce_scatter | solution.py:126
  528.8 8.5 %all-gather = f32[8,128,128]{2,1,0:T(8,128)S(1)} all-gather(f32[2,128,128]{2,1,0:T(8,128)S(1)} %pad_maximum_fusion.10), channel_id=2, replica_groups=mesh['seq'=8,'fsdp'=4] {'fsdp'}, dimensions={0}, use_global_device_ids=true | all-gather | bytes 655360 | tf_op jit(solution)/shard_map/all_gather | solution.py:109
  538.0 6.6 %fusion.10 = bf16[1,1024,1024]{2,1,0:T(8,128)(2,1)} fusion(bf16[1,1024,1024]{2,1,0:T(8,128)(2,1)} %param.8, bf16[1024,1024]{0,1:T(8,128)(2,1)} %bitcast.20, bf16[1024,1024]{1,0:T(8,128)(2,1)} %all-gather.8.cloned.1.call-done), kind=kOutput, calls=%fused_computation.18 | convolution fusion | flops 2150629376 | bytes 8388608 | tf_op jit(solution)/shard_map/dot_general | solution.py:114
  544.7 4.1 all-gather.12.cloned.1.call-done
  548.7 2.3 broadcast_multiply_fusion
  551.1 21.0 %all-gather.10.cloned.1.call-done = f32[256,1024]{1,0:T(8,128)} async-done(((f32[32,1024]{1,0:T(8,128)}), f32[256,1024]{1,0:T(8,128)}) %all-gather.10.cloned.1.call-update) | async-done | bytes 1048592 | tf_op jit(solution)/shard_map/all_gather | solution.py:130
  572.0 2.3 broadcast_multiply_fusion.1
  (59 shorter events, 20.2 us)
Async XLA Ops:
  7.2 40.6 %all-gather.8.cloned.1.call-start = ((), (), s32[]{:S(2)}) async-start(), calls=%async_computation.7 | async-start | bytes 2621440 | tf_op jit(solution)/shard_map/all_gather | solution.py:67
  7.9 76.9 %all-gather.6.cloned.1.call-start = ((), (), s32[]{:S(2)}) async-start(), calls=%async_computation.6 | async-start | bytes 2621440 | tf_op jit(solution)/shard_map/all_gather | solution.py:71
  54.7 53.6 %all-to-all-start.1 = ((bf16[1024,8,128]{2,0,1:T(8,128)(2,1)}), bf16[1024,8,128]{2,0,1:T(8,128)(2,1)S(1)}, u32[]{:S(2)}, u32[]{:S(2)}) async-start(bf16[1024,8,128]{2,0,1:T(8,128)(2,1)} %copy.26), calls=%async_computation.1 | async-start | bytes 4194304 | tf_op jit(solution)/shard_map/all_to_all | solution.py:76
  108.4 4.7 copy-start.10
  108.4 8.6 %copy-start.9 = (bf16[2,128,128]{2,1,0:T(8,128)(2,1)S(1)}, bf16[2,128,128]{2,1,0:T(8,128)(2,1)}, u32[]{:S(2)}) copy-start(bf16[2,128,128]{2,1,0:T(8,128)(2,1)} %param.10) | copy-start | bytes 196612
  108.4 53.5 %all-to-all-start = ((bf16[1024,8,128]{0,2,1:T(8,128)(2,1)}), bf16[1024,8,128]{0,2,1:T(8,128)(2,1)}, u32[]{:S(2)}, u32[]{:S(2)}) async-start(bf16[1024,8,128]{0,2,1:T(8,128)(2,1)} %bitcast.92), calls=%async_computation | async-start | bytes 4194304 | tf_op jit(solution)/shard_map/all_to_all | solution.py:77
  161.9 2.2 copy-start
  161.9 2.9 copy-start.1
  173.4 1.3 copy-start.4
  173.4 2.0 copy-start.2
  182.3 53.4 %all-to-all-start.3 = ((bf16[8,1024,128]{1,2,0:T(8,128)(2,1)}), bf16[8,1024,128]{1,2,0:T(8,128)(2,1)}, u32[]{:S(2)}, u32[]{:S(2)}) async-start(bf16[8,1024,128]{1,2,0:T(8,128)(2,1)} %bitcast.85), calls=%async_computation.3 | async-start | bytes 4194304 | tf_op jit(solution)/shard_map/all_to_all | solution.py:111
  186.6 199.8 %reduce-scatter.9.cloned.1.call-start = ((), (), s32[]{:S(2)}) async-start(), calls=%async_computation.11 | async-start | bytes 4325376 | tf_op jit(solution)/shard_map/reduce_scatter | solution.py:123
  235.7 2.2 copy-start.11
  242.2 2.5 copy-start.7
  242.2 2.5 copy-start.8
  244.7 1.2 copy-start.5
  249.7 60.8 %all-to-all-start.2 = ((bf16[8,1024,128]{1,2,0:T(8,128)(2,1)}), bf16[8,1024,128]{1,2,0:T(8,128)(2,1)}, u32[]{:S(2)}, u32[]{:S(2)}) async-start(bf16[8,1024,128]{1,2,0:T(8,128)(2,1)} %bitcast.86), calls=%async_computation.2 | async-start | bytes 4194304 | tf_op jit(solution)/shard_map/all_to_all | solution.py:112
  254.1 274.6 %reduce-scatter.7.cloned.1.call-start = ((), (), s32[]{:S(2)}) async-start(), calls=%async_computation.10 | async-start | bytes 4325376 | tf_op jit(solution)/shard_map/reduce_scatter | solution.py:126
  322.7 226.1 %all-gather.12.cloned.1.call-start = ((), (), s32[]{:S(2)}) async-start(), calls=%async_computation.9 | async-start | bytes 1179648 | tf_op jit(solution)/shard_map/all_gather | solution.py:131
  386.5 185.6 %all-gather.10.cloned.1.call-start = ((), (), s32[]{:S(2)}) async-start(), calls=%async_computation.8 | async-start | bytes 1179648 | tf_op jit(solution)/shard_map/all_gather | solution.py:130
  386.8 4.5 copy-start.3
  386.8 4.5 copy-start.6
Sparse Core Ops, SparseCore 0:
  9.8 37.8 all-gather.7
  49.6 35.1 all-gather.5
  242.3 144.0 reduce-scatter.8
  388.6 140.0 reduce-scatter.6
  530.2 18.5 all-gather.11
  550.2 21.8 all-gather.9
